TPU v7x, 128 devices: a whole 4x4x4 slice. The times are simulated.
128 devices in a mesh: dp: 16 (over y, x), tensor: 8 (over z, core).
Axes of the slice: x: 4, y: 4, z: 4, core: 2. Of those that a mesh axis runs over, the one named last changes fastest.
Arguments:
- attn_out: bfloat16 [16384, 8192], P('dp', 'tensor'), may hold values from -6 to 6
- out_weight: bfloat16 [8192, 3584], P('tensor', 'dp'), may hold values from -0.0625 to 0.0625
- residual: bfloat16 [16384, 3584], P(('dp', 'tensor')), may hold values from -101 to 101
- norm_gain: float32 [3584], replicated, may hold values from 0.5 to 1.5
- expert_ids: int32 [16384, 8], P(('dp', 'tensor')), may hold values from 0 to 127, all different within a row; in each aligned block of 128 rows (0 to 127, 128 to 255, ...) at most 12 rows name the same one
- route_weight: float32 [16384, 8], P(('dp', 'tensor')), may hold values from 0.05 to 0.35
- w_gate: bfloat16 [128, 3584, 1024], P(('dp', 'tensor')), may hold values from -1 to 1
- w_up: bfloat16 [128, 3584, 1024], P(('dp', 'tensor')), may hold values from -1 to 1
- w_down: bfloat16 [128, 1024, 3584], P(('dp', 'tensor')), may hold values from -0.1875 to 0.1875
- history_x: float32 [16], replicated, may hold values from 8 to 40
- history_h: float32 [16], replicated, may hold values from 4 to 16
Outputs:
- layer_out: bfloat16 [16384, 3584], P(('dp', 'tensor'))
- new_history_x: float32 [16], replicated
- new_history_h: float32 [16], replicated
Inputs may be any that keep to these rules, and one draw needn't show every extreme that they name: `expert_ids`: among the routes of one device's 128 tokens no expert is named more than 12 times, a bound that some block reaches.
All inputs are finite; a program needn't handle non-finite values.
Results may differ from a plain program's by a relative error of at most 0.02.
Values may be sent and summed in bfloat16 or wider, within the bound.
A program may use at most 128 MiB of HBM per device.

v0:
```python
import jax
import jax.numpy as jnp
from jax import lax
from jax.sharding import PartitionSpec as P

FP8_LIMIT = 448.0


def body(
    attn_out,
    out_weight,
    residual,
    norm_gain,
    expert_ids,
    route_weight,
    w_gate,
    w_up,
    w_down,
    history_x,
    history_h,
):
    data_count = lax.axis_size("dp")
    tensor_count = lax.axis_size("tensor")
    experts = data_count * tensor_count
    local_rows = residual.shape[0]
    width = residual.shape[1]
    top_count = expert_ids.shape[1]
    capacity = max(2, 3 * local_rows * top_count // (2 * experts))
    head_terms = jnp.dot(
        attn_out,
        lax.all_gather(out_weight, "dp", axis=1, tiled=True),
        preferred_element_type=jnp.float32,
    )
    projected = lax.psum_scatter(
        head_terms.astype(jnp.bfloat16), "tensor", scatter_dimension=0, tiled=True
    ).astype(jnp.float32)
    stream = residual.astype(jnp.float32) + projected
    normed = (
        stream * lax.rsqrt(jnp.mean(stream * stream, axis=-1, keepdims=True) + 1e-06) * norm_gain
    )
    local_peak_x = jnp.max(jnp.abs(normed))
    amax_x = lax.pmax(local_peak_x, ("dp", "tensor"))
    scale_x = FP8_LIMIT / jnp.max(history_x)
    inv_x = jnp.max(history_x) / FP8_LIMIT
    scale_h = FP8_LIMIT / jnp.max(history_h)
    inv_h = jnp.max(history_h) / FP8_LIMIT
    quantized = jnp.clip(normed * scale_x, -FP8_LIMIT, FP8_LIMIT).astype(jnp.bfloat16)
    flat_ids = expert_ids.reshape(-1)
    onehot = (flat_ids[:, None] == jnp.arange(experts, dtype=jnp.int32)[None, :]).astype(jnp.int32)
    before = jnp.cumsum(onehot, axis=0) - onehot
    slot_index = jnp.sum(before * onehot, axis=-1)
    position = flat_ids * capacity + slot_index
    matches = (
        position.reshape(local_rows, top_count)[:, :, None]
        == jnp.arange(experts * capacity, dtype=jnp.int32)[None, None, :]
    )
    placing = jnp.sum(matches.astype(jnp.int32), axis=1).astype(jnp.bfloat16)
    outgoing = lax.dot_general(
        placing, quantized, (((0,), (0,)), ((), ())), preferred_element_type=jnp.float32
    )
    outgoing = outgoing.astype(jnp.bfloat16).reshape(experts, capacity, width)
    gate_matrix = w_gate[0]
    up_matrix = w_up[0]
    down_matrix = w_down[0]
    token_block = lax.all_to_all(
        outgoing, ("dp", "tensor"), split_axis=0, concat_axis=0, tiled=True
    )
    source_count = token_block.shape[0]
    slot_count = token_block.shape[1]
    flat_rows = token_block.reshape(source_count * slot_count, width)
    gate = jnp.dot(flat_rows, gate_matrix, preferred_element_type=jnp.float32) * inv_x
    upper = jnp.dot(flat_rows, up_matrix, preferred_element_type=jnp.float32) * inv_x
    hidden = jax.nn.silu(gate) * upper
    row_peaks = jnp.max(jnp.abs(hidden), axis=1).reshape(source_count, slot_count)
    hidden_q = jnp.clip(hidden * scale_h, -FP8_LIMIT, FP8_LIMIT).astype(jnp.bfloat16)
    expert_out = (
        jnp.dot(hidden_q, down_matrix, preferred_element_type=jnp.float32) * inv_h
    ).astype(jnp.bfloat16)
    expert_out, row_peaks = (expert_out.reshape(source_count, slot_count, width), row_peaks)
    returned = lax.all_to_all(expert_out, ("dp", "tensor"), split_axis=0, concat_axis=0, tiled=True)
    returned_flat = returned.reshape(experts * capacity, width)
    picked = returned_flat[position].reshape(local_rows, top_count, width)
    mixture = jnp.sum(picked.astype(jnp.float32) * route_weight[:, :, None], axis=1)
    layer_out = (stream + mixture).astype(jnp.bfloat16)
    local_peak_h = jnp.max(row_peaks)
    amax_h = lax.pmax(local_peak_h, ("dp", "tensor"))
    new_history_x = jnp.concatenate([amax_x[None], history_x[:-1]])
    new_history_h = jnp.concatenate([amax_h[None], history_h[:-1]])
    return (layer_out, new_history_x, new_history_h)


def solution(mesh):
    in_specs = (
        P("dp", "tensor"),
        P("tensor", "dp"),
        P(("dp", "tensor"), None),
        P(),
        P(("dp", "tensor"), None),
        P(("dp", "tensor"), None),
        P(("dp", "tensor"), None, None),
        P(("dp", "tensor"), None, None),
        P(("dp", "tensor"), None, None),
        P(),
        P(),
    )
    out_specs = (P(("dp", "tensor"), None), P(), P())
    return jax.shard_map(body, mesh=mesh, in_specs=in_specs, out_specs=out_specs, check_vma=False)
```

profile of v0, /device:TPU:1, one launch (start us, length us, event | category | flops | bytes accessed | tf_op | source)
XLA Modules:
  0.0 784.3 jit_solution(17509006008396059354)
XLA Ops:
  7.2 0.0 copy-start
  7.2 0.0 all-gather.2.cloned.1.call-start
  7.2 0.7 all-gather.2.cloned.1.call-update
  7.9 0.0 reduce-scatter.2.cloned.1.call-start
  8.0 71.4 %all-gather.2.cloned.1.call-done = bf16[1024,3584]{0,1:T(8,128)(2,1)} async-done(((bf16[1024,224]{0,1:T(8,128)(2,1)}), bf16[1024,3584]{0,1:T(8,128)(2,1)}) %all-gather.2.cloned.1.call-update) | async-done | bytes 7340048 | tf_op jit(solution)/shard_map/all_gather | solution.py:31
  79.4 0.0 copy-done
  79.4 12.8 %convolution_convert_fusion.1 = bf16[1024,3584]{1,0:T(8,128)(2,1)} fusion(bf16[1024,1024]{1,0:T(8,128)(2,1)S(1)} %copy-done, bf16[1024,3584]{0,1:T(8,128)(2,1)} %all-gather.2.cloned.1.call-done), kind=kOutput, calls=%fused_computation.5 | convolution fusion | flops 7519862784 | bytes 16777216 | tf_op jit(solution)/shard_map/dot_general | solution.py:29
  92.3 0.0 reduce-scatter.2.cloned.1.call-update
  92.3 0.6 copy-done.6
  92.9 0.1 copy.22
  93.0 0.1 eq.42
  93.1 0.1 eq.38
  93.2 0.1 copy.25
  93.3 0.2 fusion.18
  93.6 0.1 copy.26
  93.7 0.4 fusion.17
  94.1 0.1 reduce_sum.41
  94.2 0.0 copy-done.9
  94.2 0.6 reduce_max.35
  95.5 2.5 convert_reduce_fusion
  98.0 41.1 %reduce-scatter.2.cloned.1.call-done = bf16[128,3584]{1,0:T(8,128)(2,1)} async-done(((bf16[1024,3584]{1,0:T(8,128)(2,1)}), bf16[128,3584]{1,0:T(8,128)(2,1)}) %reduce-scatter.2.cloned.1.call-update) | async-done | bytes 917520 | tf_op jit(solution)/shard_map/reduce_scatter | solution.py:34
  139.1 0.0 copy-done.3
  139.1 1.6 multiply_reduce_fusion
  140.7 0.0 copy-done.5
  140.7 7.1 convolution_convert_fusion
  147.8 17.1 %reshape.85 = bf16[128,12,3584]{2,1,0:T(8,128)(2,1)} reshape(bf16[1536,3584]{1,0:T(8,128)(2,1)} %convolution_convert_fusion) | data formatting | bytes 22020096 | tf_op jit(solution)/shard_map/reshape | solution.py:61
  164.9 8.8 %all-to-all-start = ((bf16[128,12,3584]{2,1,0:T(8,128)(2,1)}), bf16[128,12,3584]{2,1,0:T(8,128)(2,1)}, u32[]{:S(2)}, u32[]{:S(2)}) async-start(bf16[128,12,3584]{2,1,0:T(8,128)(2,1)} %reshape.85), calls=%async_computation.1 | async-start | bytes 29360128 | tf_op jit(solution)/shard_map/all_to_all | solution.py:65
  174.3 0.0 copy-done.8
  174.3 0.6 reduce_max.36
  176.3 190.6 %all-to-all-done = bf16[128,12,3584]{2,1,0:T(8,128)(2,1)} async-done(((bf16[128,12,3584]{2,1,0:T(8,128)(2,1)}), bf16[128,12,3584]{2,1,0:T(8,128)(2,1)}, u32[]{:S(2)}, u32[]{:S(2)}) %all-to-all-start) | async-done | bytes 11010080 | tf_op jit(solution)/shard_map/all_to_all | solution.py:65
  366.9 17.1 %reshape.86 = bf16[1536,3584]{1,0:T(8,128)(2,1)} reshape(bf16[128,12,3584]{2,1,0:T(8,128)(2,1)} %all-to-all-done) | data formatting | bytes 22020096 | tf_op jit(solution)/shard_map/reshape | solution.py:70
  384.0 16.5 %fusion.2 = f32[1536,1024]{1,0:T(8,128)S(1)} fusion(bf16[1536,3584]{1,0:T(8,128)(2,1)} %reshape.86, bf16[1,3584,1024]{2,1,0:T(8,128)(2,1)} %param.18), kind=kOutput, calls=%fused_computation.7 | convolution fusion | flops 11274289152 | bytes 24641536 | tf_op jit(solution)/shard_map/dot_general | solution.py:72
  400.6 0.0 slice-start.1
  400.6 18.3 %abs_reduce_fusion = (f32[]{:T(128)}, f32[1536,1024]{1,0:T(8,128)}) fusion(f32[1536,1024]{1,0:T(8,128)S(1)} %fusion.2, f32[]{:T(128)S(6)} %div.25, bf16[1536,3584]{1,0:T(8,128)(2,1)S(1)} %copy-done.2, bf16[1,3584,1024]{2,1,0:T(8,128)(2,1)} %param.17), kind=kOutput, calls=%fused_computation.11 | convolution fusion | flops 11288444928 | bytes 30933000 | tf_op jit(solution)/shard_map/dot_general | solution.py:71
  418.8 17.2 %multiply_convert_fusion = bf16[1536,3584]{1,0:T(8,128)(2,1)} fusion(f32[]{:T(128)S(6)} %div.28, bf16[1,1024,3584]{2,1,0:T(8,128)(2,1)S(1)} %bitcast.41, f32[1536,1024]{1,0:T(8,128)} %get-tuple-element.10, f32[]{:T(128)S(6)} %div.27), kind=kOutput, calls=%fused_computation.1 | convolution fusion | flops 11290017792 | bytes 24641544 | tf_op jit(solution)/shard_map/dot_general | solution.py:77
  436.0 17.1 %reshape.87 = bf16[128,12,3584]{2,1,0:T(8,128)(2,1)} reshape(bf16[1536,3584]{1,0:T(8,128)(2,1)} %multiply_convert_fusion) | data formatting | bytes 22020096 | tf_op jit(solution)/shard_map/reshape | solution.py:79
  453.1 11.7 %all-to-all-start.1 = ((bf16[128,12,3584]{2,1,0:T(8,128)(2,1)}), bf16[128,12,3584]{2,1,0:T(8,128)(2,1)}, u32[]{:S(2)}, u32[]{:S(2)}) async-start(bf16[128,12,3584]{2,1,0:T(8,128)(2,1)} %reshape.87), calls=%async_computation.2 | async-start | bytes 29360128 | tf_op jit(solution)/shard_map/all_to_all | solution.py:80
  464.8 0.1 mul.102
  464.9 0.0 copy-done.7
  464.9 0.1 copy.27
  465.0 191.2 %all-to-all-done.1 = bf16[128,12,3584]{2,1,0:T(8,128)(2,1)} async-done(((bf16[128,12,3584]{2,1,0:T(8,128)(2,1)}), bf16[128,12,3584]{2,1,0:T(8,128)(2,1)}, u32[]{:S(2)}, u32[]{:S(2)}) %all-to-all-start.1) | async-done | bytes 11010080 | tf_op jit(solution)/shard_map/all_to_all | solution.py:80
  656.2 17.1 %reshape.88 = bf16[1536,3584]{1,0:T(8,128)(2,1)} reshape(bf16[128,12,3584]{2,1,0:T(8,128)(2,1)} %all-to-all-done.1) | data formatting | bytes 22020096 | tf_op jit(solution)/shard_map/reshape | solution.py:81
  673.3 19.5 %gather_fusion = bf16[1024,3584]{1,0:T(8,128)(2,1)} fusion(bf16[1536,3584]{1,0:T(8,128)(2,1)} %reshape.88, s32[1024]{0:T(1024)S(1)} %broadcast_clamp_fusion), kind=kCustom, calls=%fused_computation | custom fusion | bytes 14684160 | tf_op jit(solution)/shard_map/gather | solution.py:82
  692.8 9.9 %fusion = f32[128,3584]{1,0:T(8,128)S(1)} fusion(bf16[1024,3584]{1,0:T(8,128)(2,1)} %gather_fusion, f32[128,8]{1,0:T(8,128)S(1)} %copy.27), kind=kLoop, calls=%fused_computation.4 | loop fusion | flops 10551296 | bytes 9179136 | tf_op jit(solution)/shard_map/reduce_sum | solution.py:83
  702.7 0.0 copy-done.4
  702.7 2.0 abs_reduce_fusion.1
  704.7 70.9 %all-reduce = (f32[1]{0:T(128)}, f32[1]{0:T(128)}) all-reduce(f32[1]{0:T(128)} %bitcast.9, f32[1]{0:T(128)} %bitcast.10), channel_id=1, replica_groups=mesh['dp'=16,'tensor'=8] {'dp','tensor'}, use_global_device_ids=true, to_apply=%region_10.11 | all-reduce | flops 2 | bytes 16 | tf_op jit(solution)/shard_map/pmax | solution.py:42
  775.6 1.8 pad_maximum_fusion
  (23 shorter events, 0.1 us)
Async XLA Ops:
  7.2 72.2 %copy-start = (bf16[1024,1024]{1,0:T(8,128)(2,1)S(1)}, bf16[1024,1024]{1,0:T(8,128)(2,1)}, u32[]{:S(2)}) copy-start(bf16[1024,1024]{1,0:T(8,128)(2,1)} %param.11) | copy-start | bytes 6291460
  7.2 72.2 %all-gather.2.cloned.1.call-start = ((), (), s32[]{:S(2)}) async-start(), calls=%async_computation.3 | async-start | bytes 7798784 | tf_op jit(solution)/shard_map/all_gather | solution.py:31
  7.9 131.2 %reduce-scatter.2.cloned.1.call-start = ((), (), s32[]{:S(2)}) async-start(), calls=%async_computation.4 | async-start | bytes 8257536 | tf_op jit(solution)/shard_map/reduce_scatter | solution.py:34
  92.2 0.7 copy-start.6
  92.2 1.9 copy-start.9
  92.2 46.9 %copy-start.3 = (bf16[128,3584]{1,0:T(8,128)(2,1)S(1)}, bf16[128,3584]{1,0:T(8,128)(2,1)}, u32[]{:S(2)}) copy-start(bf16[128,3584]{1,0:T(8,128)(2,1)} %param.13) | copy-start | bytes 2752516
  92.2 48.4 %copy-start.5 = (f32[3584]{0:T(1024)S(1)}, f32[3584]{0:T(1024)}, u32[]{:S(2)}) copy-start(f32[3584]{0:T(1024)} %param.14) | copy-start | bytes 43012
  164.9 9.5 %copy-start.8 = (f32[16]{0:T(128)S(1)}, f32[16]{0:T(128)}, u32[]{:S(2)}) copy-start(f32[16]{0:T(128)} %param.21) | copy-start | bytes 196
  164.9 202.0 %all-to-all-start = ((bf16[128,12,3584]{2,1,0:T(8,128)(2,1)}), bf16[128,12,3584]{2,1,0:T(8,128)(2,1)}, u32[]{:S(2)}, u32[]{:S(2)}) async-start(bf16[128,12,3584]{2,1,0:T(8,128)(2,1)} %reshape.85), calls=%async_computation.1 | async-start | bytes 29360128 | tf_op jit(solution)/shard_map/all_to_all | solution.py:65
  384.0 16.6 %copy-start.2 = (bf16[1536,3584]{1,0:T(8,128)(2,1)S(1)}, bf16[1536,3584]{1,0:T(8,128)(2,1)}, u32[]{:S(2)}) copy-start(bf16[1536,3584]{1,0:T(8,128)(2,1)} %reshape.86) | copy-start | bytes 33030148
  384.0 34.8 %slice-start = ((s8[7340032]{0:T(1024)(128)(4,1)}), s8[4194304]{0:T(1024)(128)(4,1)S(1)}, s32[]{:S(2)}) async-start(s8[7340032]{0:T(1024)(128)(4,1)} %bitcast.40), calls=%async_computation.5 | async-start | bytes 8388608
  400.6 18.3 %slice-start.1 = ((s8[7340032]{0:T(1024)(128)(4,1)}), s8[3145728]{0:T(1024)(128)(4,1)S(1)}, s32[]{:S(2)}) async-start(s8[7340032]{0:T(1024)(128)(4,1)} %bitcast.40), calls=%async_computation.6 | async-start | bytes 6291456
  453.1 11.8 %copy-start.7 = (f32[128,8]{0,1:T(8,128)S(1)}, f32[128,8]{0,1:T(8,128)}, u32[]{:S(2)}) copy-start(f32[128,8]{0,1:T(8,128)} %param.16) | copy-start | bytes 12292
  453.1 203.1 %all-to-all-start.1 = ((bf16[128,12,3584]{2,1,0:T(8,128)(2,1)}), bf16[128,12,3584]{2,1,0:T(8,128)(2,1)}, u32[]{:S(2)}, u32[]{:S(2)}) async-start(bf16[128,12,3584]{2,1,0:T(8,128)(2,1)} %reshape.87), calls=%async_computation.2 | async-start | bytes 29360128 | tf_op jit(solution)/shard_map/all_to_all | solution.py:80
  673.3 104.1 %copy-start.1 = (bf16[1024,1024]{1,0:T(8,128)(2,1)S(1)}, bf16[1024,1024]{1,0:T(8,128)(2,1)}, u32[]{:S(2)}) copy-start(bf16[1024,1024]{1,0:T(8,128)(2,1)} %param.11) | copy-start | bytes 6291460
  692.8 9.9 %copy-start.4 = (bf16[128,3584]{1,0:T(8,128)(2,1)S(1)}, bf16[128,3584]{1,0:T(8,128)(2,1)}, u32[]{:S(2)}) copy-start(bf16[128,3584]{1,0:T(8,128)(2,1)} %reduce-scatter.2.cloned.1.call-done) | copy-start | bytes 2752516
Sparse Core Ops, SparseCore 0:
  10.2 69.2 all-gather.1
  92.4 46.6 reduce-scatter.1
where the time goes:
time: 786 us; the launch traced here: 784 us
  waiting for transfers between devices  495 us (63%)
  local copies, waits for them, and re-layouts  89.4 us (11%)
  matrix products  71.9 us (9%)
  blocking collectives  70.9 us (9%)
  starting transfers between devices  20.6 us (3%)
  other arithmetic  19.6 us (2%)
  between operations  16.9 us (2%)
    all_to_all x1, waiting for transfers between devices, body(): lax.all_to_all(expert_out, ('dp', 'tensor'), split_axis=0, concat_axis=0,...  191 us
    all_to_all x1, waiting for transfers between devices, body(): lax.all_to_all(outgoing, ('dp', 'tensor'), split_axis=0, concat_axis=0, t...  191 us
    all_gather x1, waiting for transfers between devices, body(): lax.all_gather(out_weight, 'dp', axis=1, tiled=True)  71.4 us
    pmax x1, blocking collectives, body(): amax_x = lax.pmax(local_peak_x, ('dp', 'tensor'))  70.9 us
    reduce_scatter x1, waiting for transfers between devices, body(): lax.psum_scatter(head_terms.astype(jnp.bfloat16), 'tensor', scatter_dimen...  41.1 us
    gather x1, local copies, waits for them, and re-layouts, body(): picked = returned_flat[position].reshape(local_rows, top_count, width)  19.5 us
    dot_general x1, matrix products, body(): jnp.dot(flat_rows, gate_matrix, preferred_element_type=jnp.float32) * inv_x  18.3 us
    dot_general x1, matrix products, body(): jnp.dot(hidden_q, down_matrix, preferred_element_type=jnp.float32) * inv_h  17.2 us
  transfers between devices with their start and end apart: 4, of which 4 were waited for; matrix products, arithmetic and copies ran while one was open for 1% of the time, Pallas kernels for 0%

commit v1 on v0

v1 whole, which is shorter than its diff:
```python
import jax
import jax.numpy as jnp
from jax import lax
from jax.sharding import Mesh
from jax.sharding import PartitionSpec as P

FP8_LIMIT = 448.0
CHIPS = ("dp", "z")
ALL = ("dp", "z", "core")
SWAP = [(0, 1), (1, 0)]


def body(
    attn_out,
    out_weight,
    residual,
    norm_gain,
    expert_ids,
    route_weight,
    w_gate,
    w_up,
    w_down,
    history_x,
    history_h,
):
    chips = lax.axis_size("dp") * lax.axis_size("z")
    experts = 2 * chips
    core = lax.axis_index("core")
    rows = residual.shape[0]
    width = residual.shape[1]
    top = expert_ids.shape[1]
    cap = max(2, 3 * rows * top // (2 * experts))
    block = 2 * cap
    slots = chips * block

    chosen = expert_ids[:, :, None] == jnp.arange(experts, dtype=jnp.int32)[None, None, :]
    member = jnp.sum(chosen.astype(jnp.float32), axis=1)
    earlier = (
        lax.broadcasted_iota(jnp.int32, (rows, rows), 1)
        < lax.broadcasted_iota(jnp.int32, (rows, rows), 0)
    ).astype(jnp.bfloat16)
    before = jnp.dot(earlier, member.astype(jnp.bfloat16), preferred_element_type=jnp.float32)
    rank = (before + 1.0) * member
    gain = jnp.sum(jnp.where(chosen, route_weight[:, :, None], 0.0), axis=1)
    table = jnp.stack([rank, gain]).astype(jnp.bfloat16)
    other_table = lax.ppermute(table, "core", SWAP)
    table = jnp.concatenate([table, other_table], axis=1)

    column = lax.broadcasted_iota(jnp.int32, (experts, slots), 1)
    spread = (
        lax.broadcasted_iota(jnp.int32, (experts, slots), 0) == 2 * (column // block) + core
    ).astype(jnp.bfloat16)
    spread_rank = jnp.dot(table[0], spread, preferred_element_type=jnp.float32)
    spread_gain = jnp.dot(table[1], spread, preferred_element_type=jnp.float32)
    column = lax.broadcasted_iota(jnp.int32, (2 * rows, slots), 1)
    source = lax.broadcasted_iota(jnp.int32, (2 * rows, slots), 0) // rows
    source = jnp.where(core == 0, source, 1 - source)
    hit = (spread_rank == (column % cap + 1).astype(jnp.float32)) & ((column // cap) % 2 == source)
    placing = hit.astype(jnp.bfloat16)
    mixing = jnp.where(hit, spread_gain, 0.0).astype(jnp.bfloat16)

    head_terms = jnp.dot(
        attn_out,
        lax.all_gather(out_weight, "dp", axis=1, tiled=True),
        preferred_element_type=jnp.float32,
    )
    projected = lax.psum_scatter(
        head_terms.astype(jnp.bfloat16), ("z", "core"), scatter_dimension=0, tiled=True
    ).astype(jnp.float32)
    stream = residual.astype(jnp.float32) + projected
    normed = (
        stream * lax.rsqrt(jnp.mean(stream * stream, axis=-1, keepdims=True) + 1e-06) * norm_gain
    )
    peak_x = jnp.max(jnp.abs(normed))
    scale_x = FP8_LIMIT / jnp.max(history_x)
    inv_x = jnp.max(history_x) / FP8_LIMIT
    scale_h = FP8_LIMIT / jnp.max(history_h)
    inv_h = jnp.max(history_h) / FP8_LIMIT
    quantized = jnp.clip(normed * scale_x, -FP8_LIMIT, FP8_LIMIT).astype(jnp.bfloat16)
    quantized = jnp.concatenate([quantized, lax.ppermute(quantized, "core", SWAP)], axis=0)
    outgoing = lax.dot_general(
        placing, quantized, (((0,), (0,)), ((), ())), preferred_element_type=jnp.float32
    )
    outgoing = outgoing.astype(jnp.bfloat16).reshape(chips, block, width)
    tokens = lax.all_to_all(outgoing, CHIPS, split_axis=0, concat_axis=0, tiled=True)
    tokens = tokens.reshape(slots, width)

    gate = jnp.dot(tokens, w_gate[0], preferred_element_type=jnp.float32) * inv_x
    upper = jnp.dot(tokens, w_up[0], preferred_element_type=jnp.float32) * inv_x
    hidden = jax.nn.silu(gate) * upper
    peak_h = jnp.max(jnp.abs(hidden))
    lane = lax.broadcasted_iota(jnp.int32, (chips, 8, 128), 1)
    peaks = lax.all_to_all(
        jnp.where(lane == 0, peak_x, peak_h), CHIPS, split_axis=0, concat_axis=0, tiled=True
    )
    hidden_q = jnp.clip(hidden * scale_h, -FP8_LIMIT, FP8_LIMIT).astype(jnp.bfloat16)
    expert_out = (
        jnp.dot(hidden_q, w_down[0], preferred_element_type=jnp.float32) * inv_h
    ).astype(jnp.bfloat16)
    expert_out, peaks = lax.optimization_barrier((expert_out, peaks))
    peaks = jnp.max(peaks, axis=0)
    peaks = jnp.maximum(peaks, lax.ppermute(peaks, "core", SWAP))
    returned = lax.all_to_all(
        expert_out.reshape(chips, block, width), CHIPS, split_axis=0, concat_axis=0, tiled=True
    ).reshape(slots, width)
    for_other = jnp.dot(mixing[rows:], returned, preferred_element_type=jnp.float32)
    from_other = lax.ppermute(for_other.astype(jnp.bfloat16), "core", SWAP)
    mixture = jnp.dot(mixing[:rows], returned, preferred_element_type=jnp.float32)
    layer_out = (stream + mixture + from_other.astype(jnp.float32)).astype(jnp.bfloat16)
    new_history_x = jnp.concatenate([peaks[0, :1], history_x[:-1]])
    new_history_h = jnp.concatenate([peaks[1, :1], history_h[:-1]])
    return (layer_out, new_history_x, new_history_h)


def solution(mesh):
    dp, tensor = mesh.shape["dp"], mesh.shape["tensor"]
    fine = Mesh(mesh.devices.reshape(dp, tensor // 2, 2), ALL)
    in_specs = (
        P("dp", ("z", "core")),
        P(("z", "core"), "dp"),
        P(ALL, None),
        P(),
        P(ALL, None),
        P(ALL, None),
        P(ALL, None, None),
        P(ALL, None, None),
        P(ALL, None, None),
        P(),
        P(),
    )
    out_specs = (P(ALL, None), P(), P())
    return jax.shard_map(body, mesh=fine, in_specs=in_specs, out_specs=out_specs, check_vma=False)
```

time: 786 us -> 598 us (0.76)
  local copies, waits for them, and re-layouts: 89.4 us -> 2.19 us
  blocking collectives: 70.9 us -> 0 us
  waiting for transfers between devices: 495 us -> 436 us
  starting transfers between devices: 20.6 us -> 38 us
  matrix products: 71.9 us -> 87.2 us
  other arithmetic: 19.6 us -> 9.34 us
    pmax x1 -> x0, blocking collectives: 70.9 us -> none  [body(): amax_x = lax.pmax(local_peak_x, ('dp', 'tensor'))]
    reshape x4 -> x0, local copies, waits for them, and re-layouts: 68.4 us -> none  [the longest x1 17.1 us: body(): returned_flat = returned.reshape(experts * capacity, width)]
    all_to_all x2 -> x3, waiting for transfers between devices: 382 us -> 317 us  [the longest x1 171 us: body(): lax.all_to_all(outgoing, CHIPS, split_axis=0, concat_axis=0, tiled=True)]
    gather x1 -> x0, local copies, waits for them, and re-layouts: 19.5 us -> none  [body(): picked = returned_flat[position].reshape(local_rows, top_count, width)]
    dot_general x3 -> x8, matrix products: 51.9 us -> 68 us  [the longest x1 19.2 us: body(): jnp.dot(tokens, w_gate[0], preferred_element_type=jnp.float32) * inv_x]
    reduce_sum x3 -> x1, other arithmetic: 12.7 us -> 0.38 us  [body(): member = jnp.sum(chosen.astype(jnp.float32), axis=1)]
    all_to_all x2 -> x3, starting transfers between devices: 20.5 us -> 31.8 us  [the longest x1 12.8 us: body(): lax.all_to_all(jnp.where(lane == 0, peak_x, peak_h), CHIPS, split_axis=0,...]
  transfers between devices with their start and end apart: 4 -> 9, of which waited for: 4 -> 6; matrix products, arithmetic and copies ran while one was open for 1% -> 5% of each run, Pallas kernels for 0% -> 0%
where the time goes in v1:
time: 598 us; the launch traced here: 589 us
  waiting for transfers between devices  436 us (73%)
  matrix products  87.2 us (15%)
  starting transfers between devices  38 us (6%)
  between operations  16.9 us (3%)
  other arithmetic  9.34 us (2%)
    all_to_all x1, waiting for transfers between devices, body(): lax.all_to_all(outgoing, CHIPS, split_axis=0, concat_axis=0, tiled=True)  171 us
    all_to_all x1, waiting for transfers between devices, body(): lax.all_to_all(expert_out.reshape(chips, block, width), CHIPS, split_axis...  145 us
    all_gather x1, waiting for transfers between devices, body(): lax.all_gather(out_weight, 'dp', axis=1, tiled=True)  71.5 us
    reduce_scatter x1, waiting for transfers between devices, body(): lax.psum_scatter(head_terms.astype(jnp.bfloat16), ('z', 'core'), scatter_...  43.3 us
    dot_general x1, matrix products, body(): jnp.dot(tokens, w_gate[0], preferred_element_type=jnp.float32) * inv_x  19.2 us
    dot_general x1, matrix products, body(): jnp.dot(hidden_q, w_down[0], preferred_element_type=jnp.float32) * inv_h  18.2 us
    dot_general x1, matrix products, body(): upper = jnp.dot(tokens, w_up[0], preferred_element_type=jnp.float32) * inv_x  16.4 us
    all_to_all x1, starting transfers between devices, body(): lax.all_to_all(jnp.where(lane == 0, peak_x, peak_h), CHIPS, split_axis=0,...  12.8 us
  transfers between devices with their start and end apart: 9, of which 6 were waited for; matrix products, arithmetic and copies ran while one was open for 5% of the time, Pallas kernels for 0%

profile of v1, /device:TPU:1, one launch (start us, length us, event | category | flops | bytes accessed | tf_op | source)
XLA Modules:
  0.0 589.2 jit_solution(1506923758467751356)
XLA Ops:
  7.2 0.0 copy-start
  7.2 0.0 all-gather.2.cloned.1.call-start
  7.2 0.7 all-gather.2.cloned.1.call-update
  7.9 0.0 reduce-scatter.2.cloned.1.call-start
  8.0 71.5 %all-gather.2.cloned.1.call-done = bf16[1024,3584]{0,1:T(8,128)(2,1)} async-done(((bf16[1024,224]{0,1:T(8,128)(2,1)}), bf16[1024,3584]{0,1:T(8,128)(2,1)}) %all-gather.2.cloned.1.call-update) | async-done | bytes 7340048 | tf_op jit(solution)/shard_map/all_gather | solution.py:64
  79.4 12.8 %convolution_convert_fusion.1 = bf16[1024,3584]{1,0:T(8,128)(2,1)} fusion(bf16[1024,1024]{1,0:T(8,128)(2,1)S(1)} %copy-done, bf16[1024,3584]{0,1:T(8,128)(2,1)} %all-gather.2.cloned.1.call-done), kind=kOutput, calls=%fused_computation.2 | convolution fusion | flops 7519862784 | bytes 16777216 | tf_op jit(solution)/shard_map/dot_general | solution.py:62
  92.3 0.0 copy-start.4
  92.3 0.0 reduce-scatter.2.cloned.1.call-update
  92.3 0.6 copy-done.5
  92.9 0.1 copy.16
  93.0 0.0 copy-done.6
  93.0 0.1 copy.17
  93.1 0.4 convert_reduce_fusion
  93.5 0.1 fusion.19
  93.7 0.8 collective-permute-start
  94.4 0.6 reduce_max.43
  95.8 43.3 %reduce-scatter.2.cloned.1.call-done = bf16[128,3584]{1,0:T(8,128)(2,1)} async-done(((bf16[1024,3584]{1,0:T(8,128)(2,1)}), bf16[128,3584]{1,0:T(8,128)(2,1)}) %reduce-scatter.2.cloned.1.call-update) | async-done | bytes 917520 | tf_op jit(solution)/shard_map/reduce_scatter | solution.py:67
  139.1 0.0 copy-done.2
  139.1 1.6 multiply_reduce_fusion
  140.7 2.3 abs_reduce_fusion.1
  143.0 1.4 collective-permute-start.1
  144.4 0.0 collective-permute-done
  144.4 0.5 fusion.11
  145.0 1.5 collective-permute-done.1
  146.5 6.4 %convolution_convert_fusion = bf16[1536,3584]{1,0:T(8,128)(2,1)} fusion(pred[256,1536]{1,0:T(32,128)(4,1)S(1)} %fusion.11, bf16[128,3584]{1,0:T(8,128)(2,1)S(1)} %collective-permute-done.1, bf16[128,3584]{1,0:T(8,128)(2,1)S(1)} %get-tuple-element.10), kind=kOutput, calls=%fused_computation.1 | convolution fusion | flops 2827747328 | bytes 13238272 | tf_op jit(solution)/shard_map/dot_general | solution.py:81
  152.9 8.9 %all-to-all-start = ((bf16[64,24,3584]{2,1,0:T(8,128)(2,1)}), bf16[64,24,3584]{2,1,0:T(8,128)(2,1)}, u32[]{:S(2)}, u32[]{:S(2)}) async-start(bf16[64,24,3584]{2,1,0:T(8,128)(2,1)} %bitcast.39), calls=%async_computation.1 | async-start | bytes 22020096 | tf_op jit(solution)/shard_map/all_to_all | solution.py:85
  162.5 0.6 reduce_max.44
  164.4 171.5 %all-to-all-done = bf16[64,24,3584]{2,1,0:T(8,128)(2,1)} async-done(((bf16[64,24,3584]{2,1,0:T(8,128)(2,1)}), bf16[64,24,3584]{2,1,0:T(8,128)(2,1)}, u32[]{:S(2)}, u32[]{:S(2)}) %all-to-all-start) | async-done | bytes 11010080 | tf_op jit(solution)/shard_map/all_to_all | solution.py:85
  335.9 16.4 %fusion.1 = f32[1536,1024]{1,0:T(8,128)S(1)} fusion(bf16[1536,3584]{1,0:T(8,128)(2,1)} %bitcast.5, bf16[1,3584,1024]{2,1,0:T(8,128)(2,1)} %param.18), kind=kOutput, calls=%fused_computation.4 | convolution fusion | flops 11274289152 | bytes 24641536 | tf_op jit(solution)/shard_map/dot_general | solution.py:89
  352.3 19.2 %abs_reduce_fusion = (f32[]{:T(128)}, f32[1536,1024]{1,0:T(8,128)}) fusion(f32[1536,1024]{1,0:T(8,128)S(1)} %fusion.1, f32[]{:T(128)S(6)} %div.52, bf16[1536,3584]{1,0:T(8,128)(2,1)} %bitcast.5, bf16[1,3584,1024]{2,1,0:T(8,128)(2,1)} %param.17), kind=kOutput, calls=%fused_computation.8 | convolution fusion | flops 11288444928 | bytes 30933000 | tf_op jit(solution)/shard_map/dot_general | solution.py:88
  371.4 1.3 compare_select_fusion
  372.7 0.8 iota.93
  373.5 12.8 %all-to-all-start.1 = ((f32[64,8,128]{2,1,0:T(8,128)}), f32[64,8,128]{2,1,0:T(8,128)S(1)}, u32[]{:S(2)}, u32[]{:S(2)}) async-start(f32[64,8,128]{2,1,0:T(8,128)} %iota.93), calls=%async_computation.2 | async-start | bytes 524288 | tf_op jit(solution)/shard_map/all_to_all | solution.py:93
  386.4 18.2 %multiply_convert_fusion = bf16[1536,3584]{1,0:T(8,128)(2,1)} fusion(f32[]{:T(128)S(6)} %div.55, bf16[1,1024,3584]{2,1,0:T(8,128)(2,1)} %param.19, f32[1536,1024]{1,0:T(8,128)} %get-tuple-element.14, f32[]{:T(128)S(6)} %div.54), kind=kOutput, calls=%fused_computation | convolution fusion | flops 11290017792 | bytes 24641544 | tf_op jit(solution)/shard_map/dot_general | solution.py:98
  404.5 0.0 all-to-all-done.1
  404.5 10.0 %all-to-all-start.2 = ((bf16[64,24,3584]{2,1,0:T(8,128)(2,1)}), bf16[64,24,3584]{2,1,0:T(8,128)(2,1)}, u32[]{:S(2)}, u32[]{:S(2)}) async-start(bf16[64,24,3584]{2,1,0:T(8,128)(2,1)} %bitcast.40), calls=%async_computation.3 | async-start | bytes 22020096 | tf_op jit(solution)/shard_map/all_to_all | solution.py:103
  414.5 0.4 fusion.10
  415.0 145.2 %all-to-all-done.2 = bf16[64,24,3584]{2,1,0:T(8,128)(2,1)} async-done(((bf16[64,24,3584]{2,1,0:T(8,128)(2,1)}), bf16[64,24,3584]{2,1,0:T(8,128)(2,1)}, u32[]{:S(2)}, u32[]{:S(2)}) %all-to-all-start.2) | async-done | bytes 11010080 | tf_op jit(solution)/shard_map/all_to_all | solution.py:103
  560.2 5.7 convolution_convert_fusion.2
  565.9 3.9 collective-permute-start.2
  569.8 0.1 reduce_max.57
  569.8 0.1 collective-permute-start.3
  569.9 1.9 collective-permute-done.3
  571.9 0.5 fusion.46
  572.4 1.2 pad_maximum_fusion.2
  573.6 1.2 pad_maximum_fusion.3
  574.9 0.0 collective-permute-done.2
  574.9 7.5 %add_convert_fusion = bf16[128,3584]{1,0:T(8,128)(2,1)} fusion(bf16[128,3584]{1,0:T(8,128)(2,1)} %collective-permute-done.2, bf16[1536,3584]{1,0:T(8,128)(2,1)} %bitcast.10, bf16[128,3584]{1,0:T(8,128)(2,1)} %reduce-scatter.2.cloned.1.call-done, bf16[128,3584]{1,0:T(8,128)(2,1)S(1)} %copy-done.2, bf16[256,1536]{1,0:T(8,128)(2,1)} %copy-done.3), kind=kOutput, calls=%fused_computation.29 | convolution fusion | flops 1412497408 | bytes 15073280 | tf_op jit(solution)/shard_map/dot_general | solution.py:108
  (25 shorter events, 0.1 us)
Async XLA Ops:
  7.2 72.2 %copy-start = (bf16[1024,1024]{1,0:T(8,128)(2,1)S(1)}, bf16[1024,1024]{1,0:T(8,128)(2,1)}, u32[]{:S(2)}) copy-start(bf16[1024,1024]{1,0:T(8,128)(2,1)} %param.11) | copy-start | bytes 6291460
  7.2 72.2 %all-gather.2.cloned.1.call-start = ((), (), s32[]{:S(2)}) async-start(), calls=%async_computation.4 | async-start | bytes 7798784 | tf_op jit(solution)/shard_map/all_gather | solution.py:64
  7.9 131.2 %reduce-scatter.2.cloned.1.call-start = ((), (), s32[]{:S(2)}) async-start(), calls=%async_computation.5 | async-start | bytes 8257536 | tf_op jit(solution)/shard_map/reduce_scatter | solution.py:67
  92.2 0.7 copy-start.5
  92.2 0.8 copy-start.6
  92.2 2.2 copy-start.7
  92.2 46.9 %copy-start.2 = (bf16[128,3584]{1,0:T(8,128)(2,1)S(1)}, bf16[128,3584]{1,0:T(8,128)(2,1)}, u32[]{:S(2)}) copy-start(bf16[128,3584]{1,0:T(8,128)(2,1)} %param.13) | copy-start | bytes 2752516
  92.3 48.4 %copy-start.4 = (f32[3584]{0:T(1024)S(1)}, f32[3584]{0:T(1024)}, u32[]{:S(2)}) copy-start(f32[3584]{0:T(1024)} %param.14) | copy-start | bytes 43012
  93.7 50.7 %collective-permute-start = (bf16[2,128,128]{2,1,0:T(8,128)(2,1)S(1)}, bf16[2,128,128]{2,1,0:T(8,128)(2,1)S(1)}, u32[]{:S(2)}, u32[]{:S(2)}) collective-permute-start(bf16[2,128,128]{2,1,0:T(8,128)(2,1)S(1)} %pad_maximum_fusion.1), channel_id=1, source_target_pairs={{0,1},{1,0},{2,3},{3,2},{4,5},{5,4},{6,7},{7,6},{8,9},{9,8},{10,11... | collective-permute-start | bytes 196616 | tf_op jit(solution)/shard_map/ppermute | solution.py:46
  143.0 3.5 collective-permute-start.1
  152.8 9.6 %copy-start.8 = (f32[16]{0:T(128)S(1)}, f32[16]{0:T(128)}, u32[]{:S(2)}) copy-start(f32[16]{0:T(128)} %param.21) | copy-start | bytes 196
  152.9 183.0 %all-to-all-start = ((bf16[64,24,3584]{2,1,0:T(8,128)(2,1)}), bf16[64,24,3584]{2,1,0:T(8,128)(2,1)}, u32[]{:S(2)}, u32[]{:S(2)}) async-start(bf16[64,24,3584]{2,1,0:T(8,128)(2,1)} %bitcast.39), calls=%async_computation.1 | async-start | bytes 22020096 | tf_op jit(solution)/shard_map/all_to_all | solution.py:85
  373.5 31.0 %all-to-all-start.1 = ((f32[64,8,128]{2,1,0:T(8,128)}), f32[64,8,128]{2,1,0:T(8,128)S(1)}, u32[]{:S(2)}, u32[]{:S(2)}) async-start(f32[64,8,128]{2,1,0:T(8,128)} %iota.93), calls=%async_computation.2 | async-start | bytes 524288 | tf_op jit(solution)/shard_map/all_to_all | solution.py:93
  404.5 155.6 %all-to-all-start.2 = ((bf16[64,24,3584]{2,1,0:T(8,128)(2,1)}), bf16[64,24,3584]{2,1,0:T(8,128)(2,1)}, u32[]{:S(2)}, u32[]{:S(2)}) async-start(bf16[64,24,3584]{2,1,0:T(8,128)(2,1)} %bitcast.40), calls=%async_computation.3 | async-start | bytes 22020096 | tf_op jit(solution)/shard_map/all_to_all | solution.py:103
  414.9 151.0 %copy-start.3 = (bf16[256,1536]{1,0:T(8,128)(2,1)}, bf16[256,1536]{1,0:T(8,128)(2,1)S(1)}, u32[]{:S(2)}) copy-start(bf16[256,1536]{1,0:T(8,128)(2,1)S(1)} %fusion.10) | copy-start | bytes 2359300
  565.9 9.0 %collective-permute-start.2 = (bf16[128,3584]{1,0:T(8,128)(2,1)S(1)}, bf16[128,3584]{1,0:T(8,128)(2,1)}, u32[]{:S(2)}, u32[]{:S(2)}) collective-permute-start(bf16[128,3584]{1,0:T(8,128)(2,1)S(1)} %convolution_convert_fusion.2), channel_id=1, source_target_pairs={{0,1},{1,0},{2,3},{3,2},{4,5},{5,4},{6,7},{7,6},{8,9},{9,8},{10,11... | collective-permute-start | bytes 2752520 | tf_op jit(solution)/shard_map/ppermute | solution.py:107
  569.8 2.0 collective-permute-start.3
  574.9 7.5 %copy-start.1 = (bf16[1024,1024]{1,0:T(8,128)(2,1)S(1)}, bf16[1024,1024]{1,0:T(8,128)(2,1)}, u32[]{:S(2)}) copy-start(bf16[1024,1024]{1,0:T(8,128)(2,1)} %param.11) | copy-start | bytes 6291460
Sparse Core Ops, SparseCore 0:
  10.2 69.2 all-gather.1
  92.4 46.6 reduce-scatter.1

commit v2 on v1

--- a/solution.py
+++ b/solution.py
@@ -1,13 +1,278 @@
 import jax
 import jax.numpy as jnp
 from jax import lax
+from jax.experimental import pallas as pl
+from jax.experimental.pallas import tpu as pltpu
 from jax.sharding import Mesh
 from jax.sharding import PartitionSpec as P
 
 FP8_LIMIT = 448.0
-CHIPS = ("dp", "z")
-ALL = ("dp", "z", "core")
+DP = ("y", "x")
+CHIPS = ("y", "x", "z")
+ALL = ("y", "x", "z", "core")
+RING = 4
+TURNS = (1, 3, 2)
 SWAP = [(0, 1), (1, 0)]
+
+
+def project_kernel(
+    a_ref,
+    w_ref,
+    out_ref,
+    gathered,
+    pair_out,
+    pair_in,
+    own,
+    sums,
+    arrived,
+    total,
+    near_sem,
+    relay_sem,
+    gathered_sem,
+    pair_send,
+    pair_recv,
+    sum_send,
+    sum_recv,
+):
+    y, x, z, core = (lax.axis_index(name) for name in ALL)
+    shards, _, half_depth, inner = gathered.shape
+    depth = 2 * half_depth
+    token = a_ref.shape[2]
+
+    def step(position, turn):
+        return lax.rem(position + turn, RING)
+
+    def along(axis, turn):
+        if axis == "x":
+            return (y, step(x, turn), z, core)
+        if axis == "y":
+            return (step(y, turn), x, z, core)
+        return (y, x, step(z, turn), core)
+
+    sibling = (y, x, z, 1 - core)
+    mesh_id = pl.DeviceIdType.MESH
+
+    def copy(src, dst, send, recv, device):
+        return pltpu.make_async_remote_copy(
+            src_ref=src,
+            dst_ref=dst,
+            send_sem=send,
+            recv_sem=recv,
+            device_id=device,
+            device_id_type=mesh_id,
+        )
+
+    barrier = pltpu.get_barrier_semaphore()
+    for axis in ("x", "y", "z"):
+        for turn in TURNS:
+            pl.semaphore_signal(
+                barrier, inc=1, device_id=along(axis, turn), device_id_type=mesh_id
+            )
+    pl.semaphore_signal(barrier, inc=1, device_id=sibling, device_id_type=mesh_id)
+    pl.semaphore_wait(barrier, 10)
+
+    mine = y * RING + x
+
+    def near(number, half, axis):
+        return copy(
+            w_ref.at[half],
+            gathered.at[mine, half],
+            near_sem.at[half, 0 if axis == "x" else 1, number],
+            gathered_sem.at[mine, half],
+            along(axis, TURNS[number]),
+        )
+
+    for number in range(3):
+        near(number, 0, "x").start()
+        near(number, 1, "y").start()
+
+    def arrival(shard, half):
+        return copy(
+            gathered.at[shard, half],
+            gathered.at[shard, half],
+            near_sem.at[0, 0, 0],
+            gathered_sem.at[shard, half],
+            sibling,
+        )
+
+    def shard_at(turn_y, turn_x):
+        return step(y, turn_y) * RING + step(x, turn_x)
+
+    def relay(half, source, number):
+        shard = shard_at(0, source) if half == 0 else shard_at(source, 0)
+        return copy(
+            gathered.at[shard, half],
+            gathered.at[shard, half],
+            relay_sem.at[half, source - 1, number],
+            gathered_sem.at[shard, half],
+            along("y" if half == 0 else "x", TURNS[number]),
+        )
+
+    def to_sibling(i):
+        return copy(pair_out.at[i], pair_in.at[i], pair_send.at[i], pair_recv.at[i], sibling)
+
+    def to_owner(i, turn):
+        return copy(
+            sums.at[i, step(z, turn)],
+            arrived.at[i, turn - 1],
+            sum_send.at[i, turn - 1],
+            sum_recv.at[i, turn - 1],
+            along("z", turn),
+        )
+
+    def terms(block, which):
+        rows = a_ref[:, which].reshape(RING * token, inner)
+        return lax.dot_general(
+            block, rows, (((1,), (1,)), ((), ())), preferred_element_type=jnp.float32
+        )
+
+    def share(i, block):
+        pair_out[i] = terms(block, 1 - core).astype(jnp.bfloat16)
+        to_sibling(i).start()
+
+    def send_sums(i):
+        to_sibling(i).wait_recv()
+        both = (own[lax.rem(i, 2)] + pair_in[i].astype(jnp.float32)).astype(jnp.bfloat16)
+        for part in range(RING):
+            sums[i, part] = both[:, part * token : (part + 1) * token]
+        for turn in TURNS:
+            to_owner(i, turn).start()
+
+    def advance(i, shard):
+        block = gathered[shard].reshape(depth, inner)
+        share(i, block)
+        send_sums(i - 1)
+        own[lax.rem(i, 2)] = terms(block, core)
+
+    def collect(i, shard):
+        for turn in TURNS:
+            to_owner(i, turn).wait_recv()
+        value = sums[i, z].astype(jnp.float32)
+        for turn in TURNS:
+            value = value + arrived[i, turn - 1].astype(jnp.float32)
+        total[pl.ds(pl.multiple_of(shard * depth, 8), depth), :] = value
+
+    def turn_of(j):
+        return 1 + 2 * j - 3 * (j // 2)
+
+    block = w_ref[...].reshape(depth, inner)
+    share(0, block)
+    for number in range(3):
+        near(number, 0, "y").start()
+        near(number, 1, "x").start()
+    own[0] = terms(block, core)
+    for source in TURNS:
+        arrival(shard_at(0, source), 0).wait_recv()
+        for number in range(3):
+            relay(0, source, number).start()
+        arrival(shard_at(source, 0), 1).wait_recv()
+        for number in range(3):
+            relay(1, source, number).start()
+
+    def straight(j, carry):
+        turn = turn_of(j)
+        shard = shard_at(0, turn)
+        arrival(shard, 1).wait_recv()
+        advance(1 + 2 * j, shard)
+        shard = shard_at(turn, 0)
+        arrival(shard, 0).wait_recv()
+        advance(2 + 2 * j, shard)
+        return carry
+
+    lax.fori_loop(0, 3, straight, 0)
+
+    collect(0, mine)
+
+    def collect_straight(j):
+        turn = turn_of(j)
+        collect(1 + 2 * j, shard_at(0, turn))
+        collect(2 + 2 * j, shard_at(turn, 0))
+
+    def diagonal_shard(j):
+        return shard_at(turn_of(j // 3), turn_of(lax.rem(j, 3)))
+
+    def diagonal(j, carry):
+        shard = diagonal_shard(j)
+        arrival(shard, 0).wait_recv()
+        arrival(shard, 1).wait_recv()
+        advance(7 + j, shard)
+
+        @pl.when(lax.rem(j, 3) == 2)
+        def _():
+            collect_straight(j // 3)
+
+        return carry
+
+    lax.fori_loop(0, 9, diagonal, 0)
+    send_sums(shards - 1)
+
+    def collect_diagonal(j, carry):
+        collect(7 + j, diagonal_shard(j))
+        return carry
+
+    lax.fori_loop(0, 9, collect_diagonal, 0)
+
+    def turn_over(b, carry):
+        start = pl.multiple_of(b * token, token)
+        out_ref[:, pl.ds(start, token)] = total[pl.ds(start, token), :].T
+        return carry
+
+    lax.fori_loop(0, total.shape[0] // token, turn_over, 0)
+
+    for number in range(3):
+        for half in range(2):
+            near(number, half, "x").wait_send()
+            near(number, half, "y").wait_send()
+            for source in TURNS:
+                relay(half, source, number).wait_send()
+
+    def finish(i, carry):
+        to_sibling(i).wait_send()
+        for turn in TURNS:
+            to_owner(i, turn).wait_send()
+        return carry
+
+    lax.fori_loop(0, shards, finish, 0)
+
+
+def project(attn_out, out_weight):
+    inner, depth = out_weight.shape
+    shards = RING * RING
+    token = attn_out.shape[0] // (2 * RING)
+    width = shards * depth
+    vmem = pl.BlockSpec(memory_space=pltpu.VMEM)
+    dma = pltpu.SemaphoreType.DMA
+    return pl.pallas_call(
+        project_kernel,
+        out_shape=jax.ShapeDtypeStruct((token, width), jnp.float32),
+        in_specs=[vmem, vmem],
+        out_specs=vmem,
+        scratch_shapes=[
+            pltpu.VMEM((shards, 2, depth // 2, inner), jnp.bfloat16),
+            pltpu.VMEM((shards, depth, RING * token), jnp.bfloat16),
+            pltpu.VMEM((shards, depth, RING * token), jnp.bfloat16),
+            pltpu.VMEM((2, depth, RING * token), jnp.float32),
+            pltpu.VMEM((shards, RING, depth, token), jnp.bfloat16),
+            pltpu.VMEM((shards, RING - 1, depth, token), jnp.bfloat16),
+            pltpu.VMEM((width, token), jnp.float32),
+            dma((2, 2, 3)),
+            dma((2, 3, 3)),
+            dma((shards, 2)),
+            dma((shards,)),
+            dma((shards,)),
+            dma((shards, 3)),
+            dma((shards, 3)),
+        ],
+        compiler_params=pltpu.CompilerParams(
+            collective_id=0, has_side_effects=True, vmem_limit_bytes=48 << 20
+        ),
+        cost_estimate=pl.CostEstimate(
+            flops=2 * attn_out.shape[0] * inner * width,
+            bytes_accessed=2 * attn_out.size + 2 * out_weight.size + 4 * token * width,
+            transcendentals=0,
+        ),
+        name="project",
+    )(attn_out.reshape(RING, 2, token, inner), out_weight.T.reshape(2, depth // 2, inner))
 
 
 def body(
@@ -23,7 +288,7 @@
     history_x,
     history_h,
 ):
-    chips = lax.axis_size("dp") * lax.axis_size("z")
+    chips = lax.axis_size(CHIPS)
     experts = 2 * chips
     core = lax.axis_index("core")
     rows = residual.shape[0]
@@ -59,14 +324,7 @@
     placing = hit.astype(jnp.bfloat16)
     mixing = jnp.where(hit, spread_gain, 0.0).astype(jnp.bfloat16)
 
-    head_terms = jnp.dot(
-        attn_out,
-        lax.all_gather(out_weight, "dp", axis=1, tiled=True),
-        preferred_element_type=jnp.float32,
-    )
-    projected = lax.psum_scatter(
-        head_terms.astype(jnp.bfloat16), ("z", "core"), scatter_dimension=0, tiled=True
-    ).astype(jnp.float32)
+    projected = project(attn_out, out_weight)
     stream = residual.astype(jnp.float32) + projected
     normed = (
         stream * lax.rsqrt(jnp.mean(stream * stream, axis=-1, keepdims=True) + 1e-06) * norm_gain
@@ -89,17 +347,14 @@
     upper = jnp.dot(tokens, w_up[0], preferred_element_type=jnp.float32) * inv_x
     hidden = jax.nn.silu(gate) * upper
     peak_h = jnp.max(jnp.abs(hidden))
-    lane = lax.broadcasted_iota(jnp.int32, (chips, 8, 128), 1)
-    peaks = lax.all_to_all(
-        jnp.where(lane == 0, peak_x, peak_h), CHIPS, split_axis=0, concat_axis=0, tiled=True
-    )
+    lane = lax.broadcasted_iota(jnp.int32, (8, 128), 0)
+    peaks = lax.optimization_barrier(jnp.where(lane == 0, peak_x, peak_h))
+    peaks = lax.optimization_barrier(lax.all_gather(peaks, ALL))
+    mixing, peaks = lax.optimization_barrier((mixing, jnp.max(peaks, axis=0)))
     hidden_q = jnp.clip(hidden * scale_h, -FP8_LIMIT, FP8_LIMIT).astype(jnp.bfloat16)
     expert_out = (
         jnp.dot(hidden_q, w_down[0], preferred_element_type=jnp.float32) * inv_h
     ).astype(jnp.bfloat16)
-    expert_out, peaks = lax.optimization_barrier((expert_out, peaks))
-    peaks = jnp.max(peaks, axis=0)
-    peaks = jnp.maximum(peaks, lax.ppermute(peaks, "core", SWAP))
     returned = lax.all_to_all(
         expert_out.reshape(chips, block, width), CHIPS, split_axis=0, concat_axis=0, tiled=True
     ).reshape(slots, width)
@@ -113,11 +368,10 @@
 
 
 def solution(mesh):
-    dp, tensor = mesh.shape["dp"], mesh.shape["tensor"]
-    fine = Mesh(mesh.devices.reshape(dp, tensor // 2, 2), ALL)
+    fine = Mesh(mesh.devices.reshape(RING, RING, RING, 2), ALL)
     in_specs = (
-        P("dp", ("z", "core")),
-        P(("z", "core"), "dp"),
+        P(DP, ("z", "core")),
+        P(("z", "core"), DP),
         P(ALL, None),
         P(),
         P(ALL, None),

time: 598 us -> 547 us (0.915); the launches traced: 589 us -> 546 us
  waiting for transfers between devices: 436 us -> 176 us
  blocking collectives: 0 us -> 181 us
  Pallas kernels: 0 us -> 79 us
  starting transfers between devices: 38 us -> 19.7 us
  between operations: 16.9 us -> 3.5 us
  matrix products: 87.2 us -> 74.7 us
    all_gather x0 -> x1, blocking collectives: none -> 181 us  [body(): peaks = lax.optimization_barrier(lax.all_gather(peaks, ALL))]
    all_to_all x1, waiting for transfers between devices: 145 us -> 0.01 us  [body(): lax.all_to_all(expert_out.reshape(chips, block, width), CHIPS, split_axis...]
    pallas_call x0 -> x1, Pallas kernels: none -> 79 us  [project(): pl.pallas_call(project_kernel, out_shape=jax.ShapeDtypeStruct((token, wid...]
    all_gather x1 -> x0, waiting for transfers between devices: 71.5 us -> none  [body(): lax.all_gather(out_weight, 'dp', axis=1, tiled=True)]
    reduce_scatter x1 -> x0, waiting for transfers between devices: 43.3 us -> none  [body(): lax.psum_scatter(head_terms.astype(jnp.bfloat16), ('z', 'core'), scatter_...]
    all_to_all x1 -> x0, starting transfers between devices: 12.8 us -> none  [body(): lax.all_to_all(jnp.where(lane == 0, peak_x, peak_h), CHIPS, split_axis=0,...]
    dot_general x1 -> x0, matrix products: 12.8 us -> none  [body(): jnp.dot(attn_out, lax.all_gather(out_weight, 'dp', axis=1, tiled=True), p...]
  transfers between devices with their start and end apart: 9 -> 5, of which waited for: 6 -> 2; matrix products, arithmetic and copies ran while one was open for 5% -> 2% of each run, Pallas kernels for 0% -> 14%
where the time goes in v2:
time: 547 us; the launch traced here: 546 us
  blocking collectives  181 us (33%)
  waiting for transfers between devices  176 us (32%)
  Pallas kernels  79 us (14%)
  matrix products  74.7 us (14%)
  starting transfers between devices  19.7 us (4%)
  other arithmetic  7.7 us (1%)
    all_gather x1, blocking collectives, body(): peaks = lax.optimization_barrier(lax.all_gather(peaks, ALL))  181 us
    all_to_all x1, waiting for transfers between devices, body(): lax.all_to_all(outgoing, CHIPS, split_axis=0, concat_axis=0, tiled=True)  174 us
    pallas_call x1, Pallas kernels, project(): pl.pallas_call(project_kernel, out_shape=jax.ShapeDtypeStruct((token, wid...  79 us
    dot_general x1, matrix products, body(): jnp.dot(tokens, w_gate[0], preferred_element_type=jnp.float32) * inv_x  19.2 us
    dot_general x1, matrix products, body(): jnp.dot(hidden_q, w_down[0], preferred_element_type=jnp.float32) * inv_h  17.1 us
    dot_general x1, matrix products, body(): upper = jnp.dot(tokens, w_up[0], preferred_element_type=jnp.float32) * inv_x  16.5 us
  transfers between devices with their start and end apart: 5, of which 2 were waited for; matrix products, arithmetic and copies ran while one was open for 2% of the time, Pallas kernels for 14%

profile of v2, /device:TPU:1, one launch (start us, length us, event | category | flops | bytes accessed | tf_op | source)
XLA Modules:
  0.0 546.1 jit_solution(14763934886907076805)
XLA Ops:
  0.6 0.8 copy.16
  1.4 0.8 copy.17
  2.2 0.4 convert_reduce_fusion
  2.6 0.1 fusion.19
  2.8 1.5 collective-permute-start
  4.3 0.0 copy-start
  4.3 1.6 copy-done
  5.8 0.0 copy-start.1
  5.8 1.0 copy-done.1
  6.9 0.0 copy-start.2
  6.9 79.0 %project.1 = f32[128,3584]{1,0:T(8,128)S(1)} custom-call(bf16[4,2,128,1024]{3,2,1,0:T(8,128)(2,1)S(1)} %bitcast.42, bf16[2,112,1024]{2,1,0:T(8,128)(2,1)S(1)} %bitcast.43), custom_call_target="tpu_custom_call" | custom-call | flops 7516192768 | bytes 4390912 | tf_op jit(solution)/shard_map/project/pallas_call | solution.py:245
  85.9 0.0 copy-done.2
  85.9 0.3 multiply_reduce_fusion
  86.3 0.0 copy-done.5
  86.3 0.6 reduce_max.44
  87.6 0.0 copy-done.4
  87.6 1.9 abs_reduce_fusion.1
  89.5 0.8 collective-permute-start.1
  90.5 0.0 collective-permute-done
  90.5 0.5 fusion.11
  91.0 1.8 collective-permute-done.1
  92.8 7.1 %convolution_convert_fusion = bf16[1536,3584]{1,0:T(8,128)(2,1)} fusion(pred[256,1536]{1,0:T(32,128)(4,1)S(1)} %fusion.11, bf16[128,3584]{1,0:T(8,128)(2,1)} %collective-permute-done.1, bf16[128,3584]{1,0:T(8,128)(2,1)} %get-tuple-element.10), kind=kOutput, calls=%fused_computation.1 | convolution fusion | flops 2827747328 | bytes 13238272 | tf_op jit(solution)/shard_map/dot_general | solution.py:339
  100.0 7.9 %all-to-all-start = ((bf16[64,24,3584]{2,1,0:T(8,128)(2,1)}), bf16[64,24,3584]{2,1,0:T(8,128)(2,1)}, u32[]{:S(2)}, u32[]{:S(2)}) async-start(bf16[64,24,3584]{2,1,0:T(8,128)(2,1)} %bitcast.44), calls=%async_computation | async-start | bytes 22020096 | tf_op jit(solution)/shard_map/all_to_all | solution.py:343
  107.9 0.0 copy-done.6
  107.9 0.6 reduce_max.57
  110.5 174.1 %all-to-all-done = bf16[64,24,3584]{2,1,0:T(8,128)(2,1)} async-done(((bf16[64,24,3584]{2,1,0:T(8,128)(2,1)}), bf16[64,24,3584]{2,1,0:T(8,128)(2,1)}, u32[]{:S(2)}, u32[]{:S(2)}) %all-to-all-start) | async-done | bytes 11010080 | tf_op jit(solution)/shard_map/all_to_all | solution.py:343
  284.6 16.5 %fusion.1 = f32[1536,1024]{1,0:T(8,128)S(1)} fusion(bf16[1536,3584]{1,0:T(8,128)(2,1)} %bitcast.8, bf16[1,3584,1024]{2,1,0:T(8,128)(2,1)} %param.18), kind=kOutput, calls=%fused_computation.3 | convolution fusion | flops 11274289152 | bytes 24641536 | tf_op jit(solution)/shard_map/dot_general | solution.py:347
  301.1 0.0 slice-start.1
  301.1 19.2 %abs_reduce_fusion = (f32[]{:T(128)}, f32[1536,1024]{1,0:T(8,128)}) fusion(f32[1536,1024]{1,0:T(8,128)S(1)} %fusion.1, f32[]{:T(128)S(6)} %div.52, bf16[1536,3584]{1,0:T(8,128)(2,1)} %bitcast.8, bf16[1,3584,1024]{2,1,0:T(8,128)(2,1)} %param.17), kind=kOutput, calls=%fused_computation.8 | convolution fusion | flops 11288444928 | bytes 30933000 | tf_op jit(solution)/shard_map/dot_general | solution.py:346
  320.4 0.0 slice-done
  320.4 0.0 slice-done.1
  320.4 17.1 %multiply_convert_fusion = bf16[1536,3584]{1,0:T(8,128)(2,1)} fusion(f32[]{:T(128)S(6)} %div.55, bf16[1,1024,3584]{2,1,0:T(8,128)(2,1)S(1)} %bitcast.50, f32[1536,1024]{1,0:T(8,128)} %get-tuple-element.14, f32[]{:T(128)S(6)} %div.54), kind=kOutput, calls=%fused_computation | convolution fusion | flops 11290017792 | bytes 24641544 | tf_op jit(solution)/shard_map/dot_general | solution.py:356
  337.5 9.2 %all-to-all-start.1 = ((bf16[64,24,3584]{2,1,0:T(8,128)(2,1)}), bf16[64,24,3584]{2,1,0:T(8,128)(2,1)}, u32[]{:S(2)}, u32[]{:S(2)}) async-start(bf16[64,24,3584]{2,1,0:T(8,128)(2,1)} %bitcast.45), calls=%async_computation.1 | async-start | bytes 22020096 | tf_op jit(solution)/shard_map/all_to_all | solution.py:358
  346.7 1.3 fusion.10
  348.0 1.2 compare_select_fusion
  349.2 0.1 iota.93
  349.3 180.7 %all-gather = f32[1024,128]{1,0:T(8,128)S(1)} all-gather(f32[8,128]{1,0:T(8,128)S(1)} %iota.93), channel_id=2, replica_groups=mesh['y'=4,'x'=4,'z'=4,'core'=2] {'y','x','z','core'}, dimensions={0}, use_global_device_ids=true | all-gather | bytes 528384 | tf_op jit(solution)/shard_map/all_gather | solution.py:352
  530.0 0.1 reduce_max.56
  530.1 0.0 all-to-all-done.1
  530.1 0.0 copy-start.3
  530.1 5.9 %convolution_convert_fusion.1 = bf16[128,3584]{1,0:T(8,128)(2,1)S(1)} fusion(bf16[1536,3584]{1,0:T(8,128)(2,1)} %bitcast.14, bf16[256,1536]{1,0:T(8,128)(2,1)} %fusion.10), kind=kOutput, calls=%fused_computation.11 | convolution fusion | flops 1409744896 | bytes 12320768 | tf_op jit(solution)/shard_map/dot_general | solution.py:361
  536.1 0.2 collective-permute-start.2
  536.3 0.5 fusion.48
  536.8 1.2 pad_maximum_fusion.2
  538.1 1.2 pad_maximum_fusion.3
  539.3 0.0 collective-permute-done.2
  539.3 0.0 copy-done.3
  539.3 6.8 %add_convert_fusion = bf16[128,3584]{1,0:T(8,128)(2,1)} fusion(bf16[128,3584]{1,0:T(8,128)(2,1)S(1)} %collective-permute-done.2, bf16[1536,3584]{1,0:T(8,128)(2,1)} %bitcast.14, bf16[256,1536]{1,0:T(8,128)(2,1)S(1)} %copy-done.3, f32[128,3584]{1,0:T(8,128)S(1)} %project.1, bf16[128,3584]{1,0:T(8,128)(2,1)S(1)} %copy-done.2), kind=kOutput, calls=%fused_computation.28 | convolution fusion | flops 1412038656 | bytes 15990784 | tf_op jit(solution)/shard_map/dot_general | solution.py:363
  (15 shorter events, 0.1 us)
Async XLA Ops:
  2.8 87.7 %collective-permute-start = (bf16[2,128,128]{2,1,0:T(8,128)(2,1)S(1)}, bf16[2,128,128]{2,1,0:T(8,128)(2,1)S(1)}, u32[]{:S(2)}, u32[]{:S(2)}) collective-permute-start(bf16[2,128,128]{2,1,0:T(8,128)(2,1)S(1)} %pad_maximum_fusion.1), channel_id=1, source_target_pairs={{0,1},{1,0},{2,3},{3,2},{4,5},{5,4},{6,7},{7,6},{8,9},{9,8},{10,11... | collective-permute-start | bytes 196616 | tf_op jit(solution)/shard_map/ppermute | solution.py:311
  4.3 1.6 copy-start
  5.8 1.0 copy-start.1
  6.9 79.1 %copy-start.2 = (bf16[128,3584]{1,0:T(8,128)(2,1)S(1)}, bf16[128,3584]{1,0:T(8,128)(2,1)}, u32[]{:S(2)}) copy-start(bf16[128,3584]{1,0:T(8,128)(2,1)} %param.13) | copy-start | bytes 2752516
  6.9 79.4 %copy-start.5 = (f32[16]{0:T(128)S(1)}, f32[16]{0:T(128)}, u32[]{:S(2)}) copy-start(f32[16]{0:T(128)} %param.20) | copy-start | bytes 196
  6.9 80.7 %copy-start.4 = (f32[3584]{0:T(1024)S(1)}, f32[3584]{0:T(1024)}, u32[]{:S(2)}) copy-start(f32[3584]{0:T(1024)} %param.14) | copy-start | bytes 43012
  89.5 3.3 collective-permute-start.1
  100.0 7.9 %copy-start.6 = (f32[16]{0:T(128)S(1)}, f32[16]{0:T(128)}, u32[]{:S(2)}) copy-start(f32[16]{0:T(128)} %param.21) | copy-start | bytes 196
  100.0 184.6 %all-to-all-start = ((bf16[64,24,3584]{2,1,0:T(8,128)(2,1)}), bf16[64,24,3584]{2,1,0:T(8,128)(2,1)}, u32[]{:S(2)}, u32[]{:S(2)}) async-start(bf16[64,24,3584]{2,1,0:T(8,128)(2,1)} %bitcast.44), calls=%async_computation | async-start | bytes 22020096 | tf_op jit(solution)/shard_map/all_to_all | solution.py:343
  284.6 35.8 %slice-start = ((s8[7340032]{0:T(1024)(128)(4,1)}), s8[4194304]{0:T(1024)(128)(4,1)S(1)}, s32[]{:S(2)}) async-start(s8[7340032]{0:T(1024)(128)(4,1)} %bitcast.49), calls=%async_computation.2 | async-start | bytes 8388608
  301.1 19.3 %slice-start.1 = ((s8[7340032]{0:T(1024)(128)(4,1)}), s8[3145728]{0:T(1024)(128)(4,1)S(1)}, s32[]{:S(2)}) async-start(s8[7340032]{0:T(1024)(128)(4,1)} %bitcast.49), calls=%async_computation.3 | async-start | bytes 6291456
  337.5 192.6 %all-to-all-start.1 = ((bf16[64,24,3584]{2,1,0:T(8,128)(2,1)}), bf16[64,24,3584]{2,1,0:T(8,128)(2,1)}, u32[]{:S(2)}, u32[]{:S(2)}) async-start(bf16[64,24,3584]{2,1,0:T(8,128)(2,1)} %bitcast.45), calls=%async_computation.1 | async-start | bytes 22020096 | tf_op jit(solution)/shard_map/all_to_all | solution.py:358
  530.1 9.2 %copy-start.3 = (bf16[256,1536]{1,0:T(8,128)(2,1)S(1)}, bf16[256,1536]{1,0:T(8,128)(2,1)}, u32[]{:S(2)}) copy-start(bf16[256,1536]{1,0:T(8,128)(2,1)} %fusion.10) | copy-start | bytes 2359300
  536.1 3.2 collective-permute-start.2
